TPU v7x, 256 devices: a whole 4x4x8 slice. The times are simulated.
256 devices in a mesh: row: 64 (over z_hi, y, x), rep: 4 (over z_lo, core).
Axes of the slice: x: 4, y: 4, z: 8 (z_hi: 4, z_lo: 2; z = z_hi * 2 + z_lo), core: 2. Of those that a mesh axis runs over, the one named last changes fastest.
Arguments:
- features: bfloat16 [32768, 128], P('row'), may hold values from -6 to 6
- weight_one: bfloat16 [128, 128], replicated, may hold values from -0.5 to 0.5
- weight_two: bfloat16 [128, 128], replicated, may hold values from -0.5 to 0.5
- cotangent: bfloat16 [32768, 128], P('row'), may hold values from -0.03125 to 0.03125
- adj_tiles: bfloat16 [64, 64, 16, 128, 128], P('row', 'rep'), may hold values from -0.09375 to 0.09375
- tile_rows: int32 [64, 64, 16], P('row', 'rep'), may hold values from 0 to 3, as said below
- tile_cols: int32 [64, 64, 16], P('row', 'rep'), may hold values from 0 to 3
- tile_counts: int32 [64, 64], P('row', 'rep'), may hold values from 0 to 16, as said below
Outputs:
- output: bfloat16 [32768, 128], P('row')
- grad_one: float32 [128, 128], replicated
- grad_two: float32 [128, 128], replicated
Inputs may be any that keep to these rules, and one draw needn't show every extreme that they name: Only slots 0 to tile_counts[b, s] - 1 of block-row b and section s are live; the other slots carry arbitrary tiles and indices that are not part of A. Section b of block-row b holds 16 live slots; many other sections hold none. `tile_rows`: the (row, column) pairs of the slots of one block-row and section are distinct.
All inputs are finite; a program needn't handle non-finite values.
Results may differ from a plain program's by a relative error of at most 0.0065.
Values may be sent and summed in bfloat16 or wider, within the bound.
A program may use at most 192 MiB of HBM per device.

v0:
```python
from functools import partial
import jax
import jax.numpy as jnp
from jax import lax
from jax.sharding import PartitionSpec as P

TILE = 128


def gelu_value(values):
    return values * 0.5 * (1.0 + lax.erf(values * 0.7071067811865476))


def gelu_slope(values):
    normal_cdf = 0.5 * (1.0 + lax.erf(values * 0.7071067811865476))
    return normal_cdf + values * jnp.exp(-0.5 * values * values) * 0.3989422804014327


def row_contract(left, right):
    return lax.dot_general(
        left, right, (((0,), (0,)), ((), ())), preferred_element_type=jnp.float32
    )


def section_work(running, pieces, section_tiles, section_rows, section_cols, live_count):
    slot_total = section_tiles.shape[0]
    count_tiles = running.shape[0]
    sources = jnp.take(pieces, section_cols, axis=0)
    products = jnp.einsum(
        "mij,mjf->mif", section_tiles, sources, preferred_element_type=jnp.float32
    )
    live_mask = jnp.arange(slot_total, dtype=jnp.int32) < live_count
    onehot = jnp.where(
        live_mask[:, None]
        & (section_rows[:, None] == jnp.arange(count_tiles, dtype=jnp.int32)[None, :]),
        1.0,
        0.0,
    ).astype(jnp.float32)
    return running + jnp.einsum("mk,mif->kif", onehot, products, precision=lax.Precision.HIGHEST)


def propagate(tile_data, row_ids, col_ids, live_counts, own_block):
    section_total = tile_data.shape[0]
    block_rows = own_block.shape[0]
    count_tiles = block_rows // TILE
    width = own_block.shape[1]
    first_section = lax.axis_index("rep") * section_total

    def pick(section_id):
        return (
            lax.dynamic_index_in_dim(tile_data, section_id, 0, keepdims=False),
            lax.dynamic_index_in_dim(row_ids, section_id, 0, keepdims=False),
            lax.dynamic_index_in_dim(col_ids, section_id, 0, keepdims=False),
            lax.dynamic_index_in_dim(live_counts, section_id, 0, keepdims=False),
        )

    zeros = jnp.zeros((count_tiles, TILE, width), jnp.float32)
    kept_total = section_total * block_rows
    kept_base = first_section * block_rows
    empty = jnp.zeros((kept_total, width), own_block.dtype)
    piece = lax.all_gather(own_block, "row", axis=0, tiled=True)
    piece_rows = piece.shape[0]
    padding = jnp.zeros((piece_rows, width), empty.dtype)
    widened = jnp.concatenate([padding, empty, padding], axis=0)
    offset = jnp.clip(jnp.int32(0) - kept_base + piece_rows, 0, kept_total + piece_rows)
    widened = lax.dynamic_update_slice_in_dim(widened, piece, offset, 0)
    kept = widened[piece_rows : piece_rows + kept_total]
    kept = kept.reshape(section_total, count_tiles, TILE, width)

    def kept_step(section_id, running):
        pieces = lax.dynamic_index_in_dim(kept, section_id, 0, keepdims=False)
        return section_work(running, pieces, *pick(section_id))

    summed = lax.fori_loop(0, section_total, kept_step, zeros)
    return summed.reshape(block_rows, width)


def whole_sum(partial_rows):
    return lax.psum(partial_rows, "rep")


def per_device(
    features, weight_one, weight_two, cotangent, adj_tiles, tile_rows, tile_cols, tile_counts
):
    spread = partial(propagate, adj_tiles[0], tile_rows[0], tile_cols[0], tile_counts[0])
    d_two = lax.dot_general(
        cotangent, weight_two, (((1,), (1,)), ((), ())), preferred_element_type=jnp.float32
    ).astype(jnp.bfloat16)
    s_one = whole_sum(spread(features)).astype(jnp.bfloat16)
    pre_one = jnp.dot(s_one, weight_one, preferred_element_type=jnp.float32)
    hidden = gelu_value(pre_one).astype(jnp.bfloat16)
    s_two = whole_sum(spread(hidden)).astype(jnp.bfloat16)
    output = jnp.dot(s_two, weight_two, preferred_element_type=jnp.float32).astype(jnp.bfloat16)
    grad_two = lax.psum(row_contract(s_two, cotangent), "row")
    d_hidden = whole_sum(spread(d_two))
    d_pre = (d_hidden * gelu_slope(pre_one)).astype(jnp.bfloat16)
    grad_one = lax.psum(row_contract(s_one, d_pre), "row")
    return (output, grad_one, grad_two)


def solution(mesh):
    placed = (
        P("row", None),
        P(),
        P(),
        P("row", None),
        P("row", "rep", None, None, None),
        P("row", "rep", None),
        P("row", "rep", None),
        P("row", "rep"),
    )
    return jax.shard_map(
        per_device,
        mesh=mesh,
        in_specs=placed,
        out_specs=(P("row", None), P(), P()),
        check_vma=False,
    )
```

profile of v0, /device:TPU:2, one launch (start us, length us, event | category | flops | bytes accessed | tf_op | source)
XLA Modules:
  0.0 1363.7 jit_solution(14181095154365439595)
XLA Ops:
  8.1 1.6 convolution_convert_fusion
  10.6 3.9 broadcast.50
  14.4 15.8 %pad_maximum_fusion = bf16[73728,128]{1,0:T(8,128)(2,1)S(1)} fusion(bf16[32768,128]{1,0:T(8,128)(2,1)} %broadcast.50, bf16[73728]{0:T(1024)(128)(2,1)S(1)} %pad.1.clone), kind=kLoop, calls=%fused_computation.90 | loop fusion | flops 56623104 | bytes 27410432 | tf_op jit(solution)/shard_map/concatenate | solution.py:64
  30.2 6.4 copy.46
  36.6 5.8 copy-done.1
  42.4 6.5 copy.38
  48.8 73.8 %all-gather.8.cloned.1.call-done = bf16[32768,128]{1,0:T(8,128)(2,1)} async-done(((bf16[512,128]{1,0:T(8,128)(2,1)}), bf16[32768,128]{1,0:T(8,128)(2,1)}) %all-gather.8.cloned.1.call-update) | async-done | bytes 8388624 | tf_op jit(solution)/shard_map/all_gather | solution.py:61
  122.6 39.0 %dynamic_update_slice.11 = bf16[73728,128]{1,0:T(8,128)(2,1)} dynamic-update-slice(bf16[73728,128]{1,0:T(8,128)(2,1)} %copy.46, bf16[32768,128]{1,0:T(8,128)(2,1)} %all-gather.8.cloned.1.call-done, s32[]{:T(128)S(6)} %min.6, s32[]{:T(128)} %constant.163.clone.1) | dynamic-update-slice | bytes 16777220 | tf_op jit(solution)/shard_map/dynamic_update_slice | solution.py:66
  161.7 3.0 slice.20
  164.7 113.0 %while.44 = (s32[]{:T(128)}, f32[4,128,128]{2,0,1:T(4,128)S(1)}, s32[16]{0:T(128)S(1)}, s32[16,16]{1,0:T(8,128)}, bf16[16,16,128,128]{3,2,1,0:T(8,128)(2,1)}, /*...) while((s32[]{:T(128)}, f32[4,128,128]{2,0,1:T(4,128)S(1)}, ...), condition=%wide.region_7.9_spmd.clone, body=%wide.region_6.8_spmd.clone.sunk | while | flops 80086320 | bytes 4985487 | solution.py:74
  176.0 1.5 fusion.124
  183.1 1.4 fusion.124
  197.2 1.4 fusion.124
  204.3 1.4 fusion.124
  218.4 1.4 fusion.124
  232.5 1.4 fusion.124
  278.5 39.1 %dynamic_update_slice.9 = bf16[73728,128]{1,0:T(8,128)(2,1)} dynamic-update-slice(bf16[73728,128]{1,0:T(8,128)(2,1)} %copy-done.1, bf16[32768,128]{1,0:T(8,128)(2,1)} %all-gather.4.cloned.1.call-done, s32[]{:T(128)S(6)} %min.6, s32[]{:T(128)} %constant.163.clone.1) | dynamic-update-slice | bytes 16777220 | tf_op jit(solution)/shard_map/dynamic_update_slice | solution.py:66
  317.6 1.7 slice.18
  319.3 98.5 %while.42 = (s32[]{:T(128)}, f32[4,128,128]{2,0,1:T(4,128)S(1)}, s32[16]{0:T(128)S(1)}, s32[16,16]{1,0:T(8,128)}, bf16[16,16,128,128]{3,2,1,0:T(8,128)(2,1)}, /*...) while((s32[]{:T(128)}, f32[4,128,128]{2,0,1:T(4,128)S(1)}, ...), condition=%wide.region_1.3_spmd.clone, body=%wide.region_0.2_spmd.clone.sunk | while | flops 80086320 | bytes 4985487 | solution.py:74
  335.0 1.4 fusion.112
  341.1 1.4 fusion.112
  347.3 1.4 fusion.112
  417.9 21.4 %all-reduce.9 = bf16[512,128]{1,0:T(8,128)(2,1)S(1)} all-reduce(f32[512,128]{1,0:T(8,128)S(1)} %bitcast.102), channel_id=1, replica_groups=mesh['row'=64,'rep'=4] {'rep'}, use_global_device_ids=true, to_apply=%region_2.4 | all-reduce | flops 65536 | bytes 393216 | tf_op jit(solution)/shard_map/psum | solution.py:79
  440.3 1.9 fusion.69
  442.1 104.2 %all-gather.6.cloned.1.call-done = bf16[32768,128]{1,0:T(8,128)(2,1)} async-done(((bf16[512,128]{1,0:T(8,128)(2,1)}), bf16[32768,128]{1,0:T(8,128)(2,1)}) %all-gather.6.cloned.1.call-update) | async-done | bytes 8388624 | tf_op jit(solution)/shard_map/all_gather | solution.py:61
  546.3 39.1 %dynamic_update_slice.10 = bf16[73728,128]{1,0:T(8,128)(2,1)} dynamic-update-slice(bf16[73728,128]{1,0:T(8,128)(2,1)} %copy.38, bf16[32768,128]{1,0:T(8,128)(2,1)} %all-gather.6.cloned.1.call-done, s32[]{:T(128)S(6)} %min.6, s32[]{:T(128)} %constant.163.clone.1) | dynamic-update-slice | bytes 16777220 | tf_op jit(solution)/shard_map/dynamic_update_slice | solution.py:66
  585.4 1.7 slice.19
  587.2 98.5 %while.43 = (s32[]{:T(128)}, f32[4,128,128]{2,0,1:T(4,128)S(1)}, s32[16]{0:T(128)S(1)}, s32[16,16]{1,0:T(8,128)}, bf16[16,16,128,128]{3,2,1,0:T(8,128)(2,1)}, /*...) while((s32[]{:T(128)}, f32[4,128,128]{2,0,1:T(4,128)S(1)}, ...), condition=%wide.region_4.6_spmd.clone, body=%wide.region_3.5_spmd.clone.sunk | while | flops 80086320 | bytes 4985487 | solution.py:74
  685.7 21.3 %all-reduce.10 = bf16[512,128]{1,0:T(8,128)(2,1)S(1)} all-reduce(f32[512,128]{1,0:T(8,128)S(1)} %bitcast.103), channel_id=1, replica_groups=mesh['row'=64,'rep'=4] {'rep'}, use_global_device_ids=true, to_apply=%region_5.7 | all-reduce | flops 65536 | bytes 393216 | tf_op jit(solution)/shard_map/psum | solution.py:79
  708.8 645.5 %all-reduce.8.cloned.1.call-done = (f32[128,128]{1,0:T(8,128)}, f32[128,128]{1,0:T(8,128)}) async-done(((f32[128,128]{1,0:T(8,128)}, f32[128,128]{1,0:T(8,128)}), (f32[128,128]{1,0:T(8,128)}, f32[128,128]{1,0:T(8,128)})) %all-reduce.8.cloned.1.call-update) | async-done | bytes 131088 | tf_op jit(solution)/shard_map/psum | solution.py:97
  1354.2 1.5 copy.58
  1355.7 1.5 copy.59
  (457 shorter events, 300.1 us)
Async XLA Ops:
  7.2 0.9 copy-start
  7.2 115.4 %all-gather.8.cloned.1.call-start = ((), (), s32[]{:S(2)}) async-start(), calls=%async_computation.2 | async-start | bytes 8519680 | tf_op jit(solution)/shard_map/all_gather | solution.py:61
  9.7 268.8 %all-gather.4.cloned.1.call-start = ((), (), s32[]{:S(2)}) async-start(), calls=%async_computation | async-start | bytes 8519680 | tf_op jit(solution)/shard_map/all_gather | solution.py:61
  10.5 429.8 %all-reduce.6.cloned.1.call-start = ((), (), s32[]{:S(2)}) async-start(), calls=%async_computation.3 | async-start | bytes 524288 | tf_op jit(solution)/shard_map/psum | solution.py:79
  30.2 12.2 copy-start.1
  48.8 115.9 %copy-start.2 = (f32[4,128,128]{2,0,1:T(4,128)S(1)}, f32[4,128,128]{2,0,1:T(4,128)}, u32[]{:S(2)}) copy-start(f32[4,128,128]{2,0,1:T(4,128)} %custom-call.2) | copy-start | bytes 786436
  48.8 115.9 %copy-start.5 = (s32[1,16]{1,0:T(1,128)S(1)}, s32[1,16]{1,0:T(1,128)}, u32[]{:S(2)}) copy-start(s32[1,16]{1,0:T(1,128)} %param.23) | copy-start | bytes 196
  278.4 267.9 %all-gather.6.cloned.1.call-start = ((), (), s32[]{:S(2)}) async-start(), calls=%async_computation.1 | async-start | bytes 8519680 | tf_op jit(solution)/shard_map/all_gather | solution.py:61
  319.3 120.0 %copy-start.4 = (bf16[128,128]{1,0:T(8,128)(2,1)S(1)}, bf16[128,128]{1,0:T(8,128)(2,1)}, u32[]{:S(2)}) copy-start(bf16[128,128]{1,0:T(8,128)(2,1)} %param.17) | copy-start | bytes 98308
  440.2 914.0 %all-reduce.8.cloned.1.call-start = ((), (), s32[]{:S(2)}) async-start(), calls=%async_computation.4 | async-start | bytes 262144 | tf_op jit(solution)/shard_map/psum | solution.py:97
  587.2 120.8 %copy-start.3 = (bf16[128,128]{1,0:T(8,128)(2,1)S(1)}, bf16[128,128]{1,0:T(8,128)(2,1)}, u32[]{:S(2)}) copy-start(bf16[128,128]{1,0:T(8,128)(2,1)} %param.18) | copy-start | bytes 98308
Sparse Core Ops, SparseCore 0:
  11.9 110.6 all-gather.7
  125.9 113.1 all-gather.3
  278.5 46.1 all-reduce.5
  440.3 105.9 all-gather.5
  708.0 646.1 all-reduce.7
where the time goes:
time: 1370 us; the launch traced here: 1360 us
  waiting for transfers between devices  824 us (60%)
  local copies, waits for them, and re-layouts  259 us (19%)
  matrix products  141 us (10%)
  other arithmetic  80.6 us (6%)
  blocking collectives  42.8 us (3%)
  between operations  14 us (1%)
    psum x1, waiting for transfers between devices, per_device(): grad_one = lax.psum(row_contract(s_one, d_pre), 'row')  645 us
    all_gather x3, waiting for transfers between devices, propagate(): piece = lax.all_gather(own_block, 'row', axis=0, tiled=True)  178 us
    dynamic_update_slice x3, local copies, waits for them, and re-layouts, propagate(): widened = lax.dynamic_update_slice_in_dim(widened, piece, offset, 0)  117 us
    dot_general x48, matrix products, section_work(): jnp.einsum('mij,mjf->mif', section_tiles, sources, preferred_element_type...  68 us
    dot_general x48, matrix products, section_work(): jnp.einsum('mk,mif->kif', onehot, products, precision=lax.Precision.HIGHEST)  66.7 us
    psum x2, blocking collectives, whole_sum(): return lax.psum(partial_rows, 'rep')  42.8 us
    eq x48, local copies, waits for them, and re-layouts, section_work(): section_rows[:, None] == jnp.arange(count_tiles, dtype=jnp.int32)[None, :]  33.5 us
    and x48, other arithmetic, section_work(): sources = jnp.take(pieces, section_cols, axis=0)  33.4 us
  transfers between devices with their start and end apart: 5, of which 3 were waited for; matrix products, arithmetic and copies ran while one was open for 24% of the time, Pallas kernels for 0%

commit v1 on v0

--- a/solution.py
+++ b/solution.py
@@ -76,7 +76,7 @@
 
 
 def whole_sum(partial_rows):
-    return lax.psum(partial_rows, "rep")
+    return jnp.sum(lax.all_gather(partial_rows, "rep"), axis=0)
 
 
 def per_device(

time: 1370 us -> 1280 us (0.934)
  waiting for transfers between devices: 824 us -> 752 us
  blocking collectives: 42.8 us -> 0 us
  local copies, waits for them, and re-layouts: 259 us -> 276 us
    all_gather x3, waiting for transfers between devices: 178 us -> 75.8 us  [propagate(): piece = lax.all_gather(own_block, 'row', axis=0, tiled=True)]
    psum x2 -> x0, blocking collectives: 42.8 us -> none  [whole_sum(): return lax.psum(partial_rows, 'rep')]
    dynamic_slice x48, local copies, waits for them, and re-layouts: 28.1 us -> 60.8 us  [pick(): lax.dynamic_index_in_dim(live_counts, section_id, 0, keepdims=False)]
    all_gather x0 -> x3, waiting for transfers between devices: none -> 26.7 us  [whole_sum(): return jnp.sum(lax.all_gather(partial_rows, 'rep'), axis=0)]
    squeeze x48, local copies, waits for them, and re-layouts: 15.4 us -> 0.86 us  [kept_step(): pieces = lax.dynamic_index_in_dim(kept, section_id, 0, keepdims=False)]
  transfers between devices with their start and end apart: 5 -> 7, of which waited for: 3 -> 4; matrix products, arithmetic and copies ran while one was open for 24% -> 38% of each run, Pallas kernels for 0% -> 0%
where the time goes in v1:
time: 1280 us; the launch traced here: 1270 us
  waiting for transfers between devices  752 us (59%)
  local copies, waits for them, and re-layouts  276 us (22%)
  matrix products  141 us (11%)
  other arithmetic  84.9 us (7%)
  between operations  14.3 us (1%)
    psum x1, waiting for transfers between devices, per_device(): grad_one = lax.psum(row_contract(s_one, d_pre), 'row')  648 us
    dynamic_update_slice x3, local copies, waits for them, and re-layouts, propagate(): widened = lax.dynamic_update_slice_in_dim(widened, piece, offset, 0)  117 us
    all_gather x3, waiting for transfers between devices, propagate(): piece = lax.all_gather(own_block, 'row', axis=0, tiled=True)  75.8 us
    dot_general x48, matrix products, section_work(): jnp.einsum('mij,mjf->mif', section_tiles, sources, preferred_element_type...  68 us
    dot_general x48, matrix products, section_work(): jnp.einsum('mk,mif->kif', onehot, products, precision=lax.Precision.HIGHEST)  66.7 us
    dynamic_slice x48, local copies, waits for them, and re-layouts, pick(): lax.dynamic_index_in_dim(live_counts, section_id, 0, keepdims=False)  60.8 us
    eq x48, local copies, waits for them, and re-layouts, section_work(): section_rows[:, None] == jnp.arange(count_tiles, dtype=jnp.int32)[None, :]  33.5 us
    and x48, other arithmetic, section_work(): sources = jnp.take(pieces, section_cols, axis=0)  33.4 us
  transfers between devices with their start and end apart: 7, of which 4 were waited for; matrix products, arithmetic and copies ran while one was open for 38% of the time, Pallas kernels for 0%

profile of v1, /device:TPU:2, one launch (start us, length us, event | category | flops | bytes accessed | tf_op | source)
XLA Modules:
  0.0 1270.3 jit_solution(8374653240530133714)
XLA Ops:
  8.1 1.6 convolution_convert_fusion
  9.8 3.9 broadcast.50
  13.7 15.8 %pad_maximum_fusion = bf16[73728,128]{1,0:T(8,128)(2,1)S(1)} fusion(bf16[32768,128]{1,0:T(8,128)(2,1)} %broadcast.50, bf16[73728]{0:T(1024)(128)(2,1)S(1)} %pad.1.clone), kind=kLoop, calls=%fused_computation.90 | loop fusion | flops 56623104 | bytes 27410432 | tf_op jit(solution)/shard_map/concatenate | solution.py:64
  29.4 6.5 copy.46
  36.0 5.5 copy-done.1
  41.5 6.5 copy.39
  48.0 74.1 %all-gather.7.cloned.1.call-done = bf16[32768,128]{1,0:T(8,128)(2,1)} async-done(((bf16[512,128]{1,0:T(8,128)(2,1)}), bf16[32768,128]{1,0:T(8,128)(2,1)}) %all-gather.7.cloned.1.call-update) | async-done | bytes 8388624 | tf_op jit(solution)/shard_map/all_gather | solution.py:61
  122.0 39.1 %dynamic_update_slice.9 = bf16[73728,128]{1,0:T(8,128)(2,1)} dynamic-update-slice(bf16[73728,128]{1,0:T(8,128)(2,1)} %copy-done.1, bf16[32768,128]{1,0:T(8,128)(2,1)} %all-gather.7.cloned.1.call-done, s32[]{:T(128)S(6)} %min.6, s32[]{:T(128)} %constant.164.clone.1) | dynamic-update-slice | bytes 16777220 | tf_op jit(solution)/shard_map/dynamic_update_slice | solution.py:66
  161.1 1.7 slice.18
  162.8 109.0 %while.42 = (s32[]{:T(128)}, f32[4,128,128]{2,0,1:T(4,128)S(1)}, s32[16]{0:T(128)}, s32[16,16]{1,0:T(8,128)}, bf16[16,16,128,128]{3,2,1,0:T(8,128)(2,1)}, /*inde...) while((s32[]{:T(128)}, f32[4,128,128]{2,0,1:T(4,128)S(1)}, ...), condition=%wide.region_1.3_spmd.clone, body=%wide.region_0.2_spmd.clone.sunk | while | flops 80086320 | bytes 4985487 | solution.py:74
  180.4 1.4 fusion.112
  207.7 1.4 fusion.112
  221.3 1.4 fusion.112
  272.7 39.1 %dynamic_update_slice.11 = bf16[73728,128]{1,0:T(8,128)(2,1)} dynamic-update-slice(bf16[73728,128]{1,0:T(8,128)(2,1)} %copy.46, bf16[32768,128]{1,0:T(8,128)(2,1)} %all-gather.15.cloned.1.call-done, s32[]{:T(128)S(6)} %min.6, s32[]{:T(128)} %constant.164.clone.1) | dynamic-update-slice | bytes 16777220 | tf_op jit(solution)/shard_map/dynamic_update_slice | solution.py:66
  311.8 1.7 slice.20
  315.8 110.6 %while.44 = (s32[]{:T(128)}, f32[4,128,128]{2,0,1:T(4,128)S(1)}, s32[16]{0:T(128)}, s32[16,16]{1,0:T(8,128)}, bf16[16,16,128,128]{3,2,1,0:T(8,128)(2,1)}, /*inde...) while((s32[]{:T(128)}, f32[4,128,128]{2,0,1:T(4,128)S(1)}, ...), condition=%wide.region_7.9_spmd.clone, body=%wide.region_6.8_spmd.clone.sunk | while | flops 80086320 | bytes 4985487 | solution.py:74
  333.8 1.4 fusion.124
  340.7 1.4 fusion.124
  361.4 1.4 fusion.124
  396.0 1.4 fusion.124
  402.9 1.4 fusion.124
  409.8 1.4 fusion.124
  427.2 1.7 all-gather.11.cloned.1.call-done
  429.0 39.1 %dynamic_update_slice.10 = bf16[73728,128]{1,0:T(8,128)(2,1)} dynamic-update-slice(bf16[73728,128]{1,0:T(8,128)(2,1)} %copy.39, bf16[32768,128]{1,0:T(8,128)(2,1)} %all-gather.11.cloned.1.call-done, s32[]{:T(128)S(6)} %min.6, s32[]{:T(128)} %constant.164.clone.1) | dynamic-update-slice | bytes 16777220 | tf_op jit(solution)/shard_map/dynamic_update_slice | solution.py:66
  468.1 1.7 slice.19
  469.8 109.0 %while.43 = (s32[]{:T(128)}, f32[4,128,128]{2,0,1:T(4,128)S(1)}, s32[16]{0:T(128)}, s32[16,16]{1,0:T(8,128)}, bf16[16,16,128,128]{3,2,1,0:T(8,128)(2,1)}, /*inde...) while((s32[]{:T(128)}, f32[4,128,128]{2,0,1:T(4,128)S(1)}, ...), condition=%wide.region_4.6_spmd.clone, body=%wide.region_3.5_spmd.clone.sunk | while | flops 80086320 | bytes 4985487 | solution.py:74
  473.8 1.4 fusion.118
  581.9 26.7 %all-gather.13.cloned.1.call-done = f32[4,512,128]{2,1,0:T(8,128)} async-done(((f32[1,512,128]{2,1,0:T(8,128)}), f32[4,512,128]{2,1,0:T(8,128)}) %all-gather.13.cloned.1.call-update) | async-done | bytes 1048592 | tf_op jit(solution)/shard_map/all_gather | solution.py:79
  610.7 1.6 convolution_convert_fusion.1
  612.3 648.2 %all-reduce.3.cloned.1.call-done = (f32[128,128]{1,0:T(8,128)}, f32[128,128]{1,0:T(8,128)}) async-done(((f32[128,128]{1,0:T(8,128)}, f32[128,128]{1,0:T(8,128)}), (f32[128,128]{1,0:T(8,128)}, f32[128,128]{1,0:T(8,128)})) %all-reduce.3.cloned.1.call-update) | async-done | bytes 131088 | tf_op jit(solution)/shard_map/psum | solution.py:97
  1260.5 1.5 copy.55
  1262.0 1.5 copy.56
  (460 shorter events, 322.0 us)
Async XLA Ops:
  7.2 0.9 copy-start
  7.2 114.9 %all-gather.7.cloned.1.call-start = ((), (), s32[]{:S(2)}) async-start(), calls=%async_computation | async-start | bytes 8519680 | tf_op jit(solution)/shard_map/all_gather | solution.py:61
  7.9 264.8 %all-gather.15.cloned.1.call-start = ((), (), s32[]{:S(2)}) async-start(), calls=%async_computation.4 | async-start | bytes 8519680 | tf_op jit(solution)/shard_map/all_gather | solution.py:61
  9.7 303.8 %all-gather.9.cloned.1.call-start = ((), (), s32[]{:S(2)}) async-start(), calls=%async_computation.1 | async-start | bytes 1310720 | tf_op jit(solution)/shard_map/all_gather | solution.py:79
  29.4 12.1 copy-start.1
  272.6 156.4 %all-gather.11.cloned.1.call-start = ((), (), s32[]{:S(2)}) async-start(), calls=%async_computation.2 | async-start | bytes 8519680 | tf_op jit(solution)/shard_map/all_gather | solution.py:61
  272.7 42.2 %copy-start.3 = (bf16[128,128]{1,0:T(8,128)(2,1)S(1)}, bf16[128,128]{1,0:T(8,128)(2,1)}, u32[]{:S(2)}) copy-start(bf16[128,128]{1,0:T(8,128)(2,1)} %param.17) | copy-start | bytes 98308
  315.8 263.8 %all-gather.17.cloned.1.call-start = ((), (), s32[]{:S(2)}) async-start(), calls=%async_computation.5 | async-start | bytes 1310720 | tf_op jit(solution)/shard_map/all_gather | solution.py:79
  427.2 181.4 %all-gather.13.cloned.1.call-start = ((), (), s32[]{:S(2)}) async-start(), calls=%async_computation.3 | async-start | bytes 1310720 | tf_op jit(solution)/shard_map/all_gather | solution.py:79
  469.8 111.2 %copy-start.2 = (f32[512,128]{1,0:T(8,128)S(1)}, f32[512,128]{1,0:T(8,128)}, u32[]{:S(2)}) copy-start(f32[512,128]{1,0:T(8,128)} %get-tuple-element.502) | copy-start | bytes 786436
  579.6 680.9 %all-reduce.3.cloned.1.call-start = ((), (), s32[]{:S(2)}) async-start(), calls=%async_computation.6 | async-start | bytes 262144 | tf_op jit(solution)/shard_map/psum | solution.py:97
Sparse Core Ops, SparseCore 0:
  11.3 110.6 all-gather.6
  125.9 113.0 all-gather.14
  272.7 28.7 all-gather.8
  315.9 113.0 all-gather.10
  430.6 28.8 all-gather.16
  579.7 28.8 all-gather.12
  611.8 648.6 all-reduce.2
